TPU v7x, 32 devices: a whole 2x2x4 slice. The times are simulated.
32 devices in a mesh: tm: 8 (over y, x, core), band: 4 (over z).
Axes of the slice: x: 2, y: 2, z: 4, core: 2. Of those that a mesh axis runs over, the one named last changes fastest.
Arguments:
- voltages: bfloat16 [4, 2, 1024, 16384], P('band', None, None, 'tm'), may hold values from -6 to 6
- antenna_flags: int32 [4, 64, 1024], P('band', 'tm'), may hold values from 0 to 1, as said below
- channel_flags: int32 [4, 64], P('band', 'tm'), may hold values from 0 to 1, as said below
Outputs:
- running_vis: float32 [4, 8, 1024, 1024], P('band', 'tm')
- dump_vis: float32 [4, 1024, 1024], P('band', 'tm')
- kurtosis: float32 [4, 1024], P('band', 'tm')
Inputs may be any that keep to these rules, and one draw needn't show every extreme that they name: `antenna_flags`: in the first flag interval of every segment of 8 intervals no signal input is dropped. `channel_flags`: every channel is kept in the first flag interval of at least one segment.
All inputs are finite; a program needn't handle non-finite values.
Results may differ from a plain program's by a relative error of at most 0.0003.
Values sent between devices are 32-bit elements; how exact they have to be, the bound alone decides.
A program may use at most 192 MiB of HBM per device.

v0:
```python
import jax
import jax.numpy as jnp
from jax import lax
from jax.sharding import PartitionSpec as P


def prefix(part, axis, combine, identity):
    place = lax.axis_index(axis)
    gathered = lax.all_gather(part, axis)
    state = jnp.zeros_like(part) + jnp.asarray(identity, part.dtype)

    def one(lap, state):
        return combine(state, lax.dynamic_index_in_dim(gathered, lap, 0, False))

    return lax.fori_loop(0, place, one, state)


def add_terms(earlier, later):
    return jax.tree.map(jnp.add, earlier, later)


def per_device(voltages, antenna_flags, channel_flags):
    time_devices = lax.axis_size("tm")
    local_volts = voltages[0]
    _, signals, samples = local_volts.shape
    intervals = antenna_flags.shape[1]
    segment_length = samples // intervals
    total_samples = samples * time_devices
    keep_weight = channel_flags[0][:, None] * antenna_flags[0]
    keep_weight = jnp.swapaxes(keep_weight, 0, 1)
    shaped = local_volts.reshape(2, signals, intervals, segment_length)
    masked = (shaped * keep_weight[None, :, :, None].astype(jnp.bfloat16)).reshape(
        2, signals, samples
    )
    real_part = jnp.einsum("rst,rut->su", masked, masked, preferred_element_type=jnp.float32)
    cross_term = jnp.einsum("st,ut->su", masked[1], masked[0], preferred_element_type=jnp.float32)
    imag_part = cross_term - jnp.swapaxes(cross_term, 0, 1)
    row_ids = jnp.arange(signals, dtype=jnp.int32)
    upper_half = row_ids[:, None] <= row_ids[None, :]
    gram_block = jnp.where(upper_half, real_part, imag_part) / total_samples
    real_volts = masked[0].astype(jnp.float32)
    imag_volts = masked[1].astype(jnp.float32)
    energy = real_volts * real_volts + imag_volts * imag_volts
    moment_one = jnp.sum(energy, axis=-1)
    moment_two = jnp.sum(energy * energy, axis=-1)
    valid_count = jnp.sum(keep_weight.astype(jnp.float32), axis=-1) * segment_length
    earlier = prefix(gram_block, "tm", add_terms, jnp.zeros_like(gram_block))
    running = earlier + gram_block
    sums_one, sums_two, counts = lax.psum((moment_one, moment_two, valid_count), "tm")
    row_count = signals // time_devices
    row_start = lax.axis_index("tm") * row_count
    dump_rows = lax.psum_scatter(gram_block, "tm", scatter_dimension=0, tiled=True)
    share_one = lax.dynamic_slice_in_dim(sums_one, row_start, row_count, 0)
    share_two = lax.dynamic_slice_in_dim(sums_two, row_start, row_count, 0)
    share_count = lax.dynamic_slice_in_dim(counts, row_start, row_count, 0)
    kurtosis = (
        (share_count + 1.0)
        / (share_count - 1.0)
        * (share_count * share_two / (share_one * share_one) - 1.0)
    )
    return (running[None, None], dump_rows[None], kurtosis[None])


def solution(mesh):
    return jax.shard_map(
        per_device,
        mesh=mesh,
        in_specs=(P("band", None, None, "tm"), P("band", "tm", None), P("band", "tm")),
        out_specs=(P("band", "tm", None, None), P("band", "tm", None), P("band", "tm")),
        check_vma=False,
    )
```

profile of v0, /device:TPU:31, one launch (start us, length us, event | category | flops | bytes accessed | tf_op | source)
XLA Modules:
  0.0 302.7 jit_solution(9306891246145146207)
XLA Ops:
  7.2 0.8 fusion.20
  8.2 1.2 mul.63
  9.5 3.4 %copy.12 = bf16[128,8,8,256]{3,1,2,0:T(8,128)(2,1)} copy(bf16[128,8,8,256]{3,2,1,0:T(8,128)(2,1)S(1)} %bitcast.50) | data formatting | bytes 8388608
  12.9 11.8 %copy.9 = bf16[1,2,1024,2048]{2,3,1,0:T(8,128)(2,1)} copy(bf16[1,2,1024,2048]{3,2,1,0:T(8,128)(2,1)} %param.5) | data formatting | bytes 16777216 | tf_op args[0]
  24.7 11.6 %copy.10 = bf16[2,1024,8,256]{3,1,2,0:T(8,128)(2,1)} copy(bf16[2,1024,8,256]{1,3,2,0:T(8,128)(2,1)} %bitcast.49) | data formatting | bytes 16777216 | tf_op jit(solution)/shard_map/reshape;squeeze | solution.py:31
  36.3 4.7 %broadcast_multiply_fusion = bf16[2,1024,8,256]{3,1,2,0:T(8,128)(2,1)S(1)} fusion(bf16[2,1024,8,256]{3,1,2,0:T(8,128)(2,1)} %copy.10, bf16[1024,8]{0,1:T(8,128)(2,1)S(1)} %fusion.20), kind=kLoop, calls=%fused_computation.14 | loop fusion | flops 4194304 | bytes 16793600 | tf_op jit(solution)/shard_map/mul | solution.py:32
  41.0 3.2 %copy-done = bf16[2,1024,8,256]{3,1,2,0:T(8,128)(2,1)} copy-done((bf16[2,1024,8,256]{3,1,2,0:T(8,128)(2,1)}, bf16[2,1024,8,256]{3,1,2,0:T(8,128)(2,1)S(1)}, u32[]{:S(2)}) %copy-start) | copy-done | bytes 8388632
  44.2 6.0 %fusion.14 = f32[1024,1024]{1,0:T(8,128)} fusion(bf16[2,1024,8,256]{3,1,2,0:T(8,128)(2,1)S(1)} %broadcast_multiply_fusion), kind=kOutput, calls=%fused_computation.19 | convolution fusion | flops 4294967296 | bytes 12582912 | tf_op jit(solution)/shard_map/st,ut->su/dot_general | solution.py:36
  50.3 5.3 %copy.11 = f32[1024,1024]{0,1:T(8,128)} copy(f32[1024,1024]{1,0:T(8,128)} %fusion.14) | data formatting | bytes 8388608 | tf_op jit(solution)/shard_map/st,ut->su/dot_general | solution.py:36
  55.6 19.8 %fusion.5 = f32[1024,1024]{1,0:T(8,128)} fusion(f32[1024,1024]{1,0:T(8,128)} %fusion.14, f32[1024,1024]{0,1:T(8,128)} %copy.11, bf16[1,2,1024,2048]{3,2,1,0:T(8,128)(2,1)} %param.5, bf16[1024,2048]{1,0:T(8,128)(2,1)} %bitcast.52), kind=kOutput, calls=%fused_computation.9 | convolution fusion | flops 8598323200 | bytes 25165824 | tf_op jit(solution)/shard_map/rst,rut->su/dot_general | solution.py:35
  75.4 0.7 reduce-scatter.2.cloned.1.call-update
  76.2 4.7 %multiply_reduce_fusion = (f32[1024]{0:T(1024)S(1)}, f32[1024]{0:T(1024)S(1)}) fusion(bf16[2,1024,8,256]{3,1,2,0:T(8,128)(2,1)} %copy-done), kind=kLoop, calls=%fused_computation.3 | loop fusion | flops 16775168 | bytes 8396800 | tf_op jit(solution)/shard_map/reduce_sum | solution.py:45
  80.9 22.9 %all-reduce = (f32[1024]{0:T(1024)S(1)}, f32[1024]{0:T(1024)S(1)}, f32[1024]{0:T(1024)S(1)}) all-reduce(f32[1024]{0:T(1024)S(1)} %get-tuple-element.28, f32[1024]{0:T(1024)S(1)} %get-tuple-element.27, f32[1024]{0:T(1024)S(1)} %broadcast_multiply_fusion.1), channel_id=1, replica_groups=mesh['tm'=8,'band'=4] {'tm'}, use_global_device_ids=true, to_apply=%region_8.9 | all-reduce | flops 3072 | bytes 24576 | tf_op jit(solution)/shard_map/psum | solution.py:49
  104.5 132.3 %all-gather.3.cloned.1.call-done = f32[8192,1024]{1,0:T(8,128)} async-done(((f32[1024,1024]{1,0:T(8,128)}), f32[8192,1024]{1,0:T(8,128)}) %all-gather.3.cloned.1.call-update) | async-done | bytes 33554448 | tf_op jit(solution)/shard_map/all_gather | solution.py:9
  236.8 2.5 broadcast_in_dim.15
  239.3 49.6 %while.10 = (s32[]{:T(128)}, f32[1024,1024]{1,0:T(8,128)}, s32[]{:T(128)}, f32[8,1024,1024]{2,1,0:T(8,128)}, s32[]{:T(128)}, /*index=5*/s32[]{:T(128)}, s32[]{:T(128)}) while((s32[]{:T(128)}, f32[1024,1024]{1,0:T(8,128)}, s32[]{:T(128)}, f32[8,1024,1024]{2,1,0:T(8,128)}, s32[]{:T(128)}, /*index=5*/s32[]{:T(128)}, s32[]{:T(128)}) %tuple.30), condition=%wide.region_1.2_spmd, body=%wide.region_0.1_spmd.sunk | while | flops 1048581 | bytes 12583035 | solution.py:15
  239.3 6.8 %bitcast_add_fusion.2 = f32[1024,1024]{1,0:T(8,128)} fusion(f32[1024,1024]{1,0:T(8,128)} %get-tuple-element.74, f32[8,1024,1024]{2,1,0:T(8,128)} %get-tuple-element.83, s32[]{:T(128)S(6)} %select_n.19), kind=kLoop, calls=%fused_computation.clone.1 | loop fusion | flops 1048576 | bytes 12582916 | tf_op jit(solution)/shard_map/while/body/add | solution.py:19
  246.2 7.6 %bitcast_add_fusion.2 = f32[1024,1024]{1,0:T(8,128)} fusion(f32[1024,1024]{1,0:T(8,128)} %get-tuple-element.74, f32[8,1024,1024]{2,1,0:T(8,128)} %get-tuple-element.83, s32[]{:T(128)S(6)} %select_n.19), kind=kLoop, calls=%fused_computation.clone.1 | loop fusion | flops 1048576 | bytes 12582916 | tf_op jit(solution)/shard_map/while/body/add | solution.py:19
  253.7 7.2 %bitcast_add_fusion.2 = f32[1024,1024]{1,0:T(8,128)} fusion(f32[1024,1024]{1,0:T(8,128)} %get-tuple-element.74, f32[8,1024,1024]{2,1,0:T(8,128)} %get-tuple-element.83, s32[]{:T(128)S(6)} %select_n.19), kind=kLoop, calls=%fused_computation.clone.1 | loop fusion | flops 1048576 | bytes 12582916 | tf_op jit(solution)/shard_map/while/body/add | solution.py:19
  260.9 7.0 %bitcast_add_fusion.2 = f32[1024,1024]{1,0:T(8,128)} fusion(f32[1024,1024]{1,0:T(8,128)} %get-tuple-element.74, f32[8,1024,1024]{2,1,0:T(8,128)} %get-tuple-element.83, s32[]{:T(128)S(6)} %select_n.19), kind=kLoop, calls=%fused_computation.clone.1 | loop fusion | flops 1048576 | bytes 12582916 | tf_op jit(solution)/shard_map/while/body/add | solution.py:19
  267.9 6.9 %bitcast_add_fusion.2 = f32[1024,1024]{1,0:T(8,128)} fusion(f32[1024,1024]{1,0:T(8,128)} %get-tuple-element.74, f32[8,1024,1024]{2,1,0:T(8,128)} %get-tuple-element.83, s32[]{:T(128)S(6)} %select_n.19), kind=kLoop, calls=%fused_computation.clone.1 | loop fusion | flops 1048576 | bytes 12582916 | tf_op jit(solution)/shard_map/while/body/add | solution.py:19
  274.8 6.9 %bitcast_add_fusion.2 = f32[1024,1024]{1,0:T(8,128)} fusion(f32[1024,1024]{1,0:T(8,128)} %get-tuple-element.74, f32[8,1024,1024]{2,1,0:T(8,128)} %get-tuple-element.83, s32[]{:T(128)S(6)} %select_n.19), kind=kLoop, calls=%fused_computation.clone.1 | loop fusion | flops 1048576 | bytes 12582916 | tf_op jit(solution)/shard_map/while/body/add | solution.py:19
  281.7 7.2 %bitcast_add_fusion.2 = f32[1024,1024]{1,0:T(8,128)} fusion(f32[1024,1024]{1,0:T(8,128)} %get-tuple-element.74, f32[8,1024,1024]{2,1,0:T(8,128)} %get-tuple-element.83, s32[]{:T(128)S(6)} %select_n.19), kind=kLoop, calls=%fused_computation.clone.1 | loop fusion | flops 1048576 | bytes 12582916 | tf_op jit(solution)/shard_map/while/body/add | solution.py:19
  288.9 7.0 %add_bitcast_fusion = f32[1,1,1024,1024]{3,2,1,0:T(8,128)} fusion(f32[1024,1024]{1,0:T(8,128)} %get-tuple-element.26, f32[1024,1024]{1,0:T(8,128)} %fusion.5), kind=kLoop, calls=%fused_computation.13 | loop fusion | flops 1048576 | bytes 12582912 | tf_op jit(solution)/shard_map/broadcast_in_dim | solution.py:61
  (13 shorter events, 1.0 us)
Async XLA Ops:
  7.2 229.6 %all-gather.3.cloned.1.call-start = ((), (), s32[]{:S(2)}) async-start(), calls=%async_computation.2 | async-start | bytes 37748736 | tf_op jit(solution)/shard_map/all_gather | solution.py:9
  41.0 3.2 %copy-start = (bf16[2,1024,8,256]{3,1,2,0:T(8,128)(2,1)}, bf16[2,1024,8,256]{3,1,2,0:T(8,128)(2,1)S(1)}, u32[]{:S(2)}) copy-start(bf16[2,1024,8,256]{3,1,2,0:T(8,128)(2,1)S(1)} %broadcast_multiply_fusion) | copy-start | bytes 25165828
  75.3 0.8 copy-start.1
  75.3 0.8 copy-start.2
  75.4 220.5 %reduce-scatter.2.cloned.1.call-start = ((), (), s32[]{:S(2)}) async-start(), calls=%async_computation.1 | async-start | bytes 4718592 | tf_op jit(solution)/shard_map/reduce_scatter | solution.py:52
Sparse Core Ops, SparseCore 0:
  75.5 161.2 all-gather.2
  240.7 50.5 reduce-scatter.1
where the time goes:
time: 304 us; the launch traced here: 303 us
  waiting for transfers between devices  133 us (44%)
  other arithmetic  67.4 us (22%)
  local copies, waits for them, and re-layouts  39.3 us (13%)
  matrix products  25.8 us (8%)
  blocking collectives  22.9 us (8%)
  between operations  14.1 us (5%)
    all_gather x1, waiting for transfers between devices, prefix(): gathered = lax.all_gather(part, axis)  132 us
    add x7, other arithmetic, add_terms(): return jax.tree.map(jnp.add, earlier, later)  49.6 us
    psum x1, blocking collectives, per_device(): lax.psum((moment_one, moment_two, valid_count), 'tm')  22.9 us
    dot_general x1, matrix products, per_device(): jnp.einsum('rst,rut->su', masked, masked, preferred_element_type=jnp.floa...  19.8 us
    unnamed x8, local copies, waits for them, and re-layouts  18.4 us
    another operation x1, local copies, waits for them, and re-layouts, per_device(): shaped = local_volts.reshape(2, signals, intervals, segment_length)  11.6 us
    broadcast_in_dim x2, other arithmetic, per_device(): return (running[None, None], dump_rows[None], kurtosis[None])  7.55 us
  transfers between devices with their start and end apart: 2, of which 1 were waited for; matrix products, arithmetic and copies ran while one was open for 21% of the time, Pallas kernels for 0%

commit v1 on v0

v1 whole, which is shorter than its diff:
```python
import functools

import jax
import jax.numpy as jnp
from jax import lax
from jax.experimental import pallas as pl
from jax.experimental.pallas import tpu as pltpu
from jax.sharding import PartitionSpec as P

MESH = pl.DeviceIdType.MESH
STEPS = 32


def chain_kernel(
    n, gram, stats, run_out, dump_out, kurt_out,
    partner, earlier, first, second, stats_in,
    x_send, x_recv, c_send, c_recv, p_send, p_recv, o_sem, d_send, d_recv, s_send, s_recv,
):
    me = lax.axis_index("tm")
    chips = n // 2
    chip, core = me // 2, me % 2
    other = chip * 2 + (1 - core)
    rows = gram.shape[0] // n
    step_rows = chips * rows // STEPS
    per_slab = rows // step_rows
    last = chips - 1

    def at(q, parity):
        slab, part = q // per_slab, q % per_slab
        return pl.ds(pl.multiple_of((slab * 2 + parity) * rows + part * step_rows, 8), step_rows)

    def flat(q):
        return pl.ds(pl.multiple_of(q * step_rows, 8), step_rows)

    def exchange(q):
        return pltpu.make_async_remote_copy(
            gram.at[at(q, 1 - core)], partner.at[flat(q)], x_send.at[q], x_recv.at[q],
            device_id={"tm": other}, device_id_type=MESH)

    def onward(q, to):
        return pltpu.make_async_remote_copy(
            second.at[flat(q)], earlier.at[flat(q)], c_send.at[q], c_recv.at[q],
            device_id={"tm": to}, device_id_type=MESH)

    def hand_over(q, source, parity):
        return pltpu.make_async_remote_copy(
            source.at[flat(q)], run_out.at[at(q, parity)], p_send.at[q], p_recv.at[q],
            device_id={"tm": other}, device_id_type=MESH)

    def keep_own(q, source):
        return pltpu.make_async_copy(source.at[flat(q)], run_out.at[at(q, core)], o_sem.at[q])

    def dump_rows(q):
        return pl.ds(pl.multiple_of((q % per_slab) * step_rows, 8), step_rows)

    def dump_send(q):
        return pltpu.make_async_remote_copy(
            second.at[flat(q)], dump_out.at[dump_rows(q)], d_send.at[q], d_recv.at[q % per_slab],
            device_id={"tm": (q // per_slab) * 2 + core}, device_id_type=MESH)

    def dump_keep(q):
        return pltpu.make_async_copy(second.at[flat(q)], dump_out.at[dump_rows(q)], d_send.at[q])

    def stat_copy(o):
        to = lax.rem(me + o, n)
        return pltpu.make_async_remote_copy(
            stats.at[to], stats_in.at[o], s_send.at[o], s_recv.at[o],
            device_id={"tm": to}, device_id_type=MESH)

    barrier = pltpu.get_barrier_semaphore()
    for o in range(1, n):
        pl.semaphore_signal(barrier, inc=1, device_id={"tm": lax.rem(me + o, n)}, device_id_type=MESH)
    pl.semaphore_wait(barrier, n - 1)

    @pl.loop(0, STEPS)
    def _(q):
        exchange(q).start()

    for o in range(1, n):
        stat_copy(o).start()

    @pl.loop(0, STEPS)
    def _(q):
        exchange(q).wait_recv()
        mine = gram[at(q, core)]
        theirs = partner[flat(q)]
        low = jnp.where(core == 0, mine, theirs)

        @pl.when(chip > 0)
        def _():
            onward(q, me).wait_recv()
            first[flat(q)] = earlier[flat(q)] + low

        @pl.when(chip == 0)
        def _():
            first[flat(q)] = low

        second[flat(q)] = first[flat(q)] + jnp.where(core == 0, theirs, mine)

        @pl.when(chip < last)
        def _():
            onward(q, me + 2).start()

        @pl.when(chip == last)
        def _():
            @pl.when(q // per_slab < last)
            def _():
                dump_send(q).start()

            @pl.when(q // per_slab == last)
            def _():
                dump_keep(q).start()

        @pl.when(core == 0)
        def _():
            hand_over(q, second, 0).start()
            keep_own(q, first).start()

        @pl.when(core == 1)
        def _():
            hand_over(q, first, 1).start()
            keep_own(q, second).start()

    total = stats[me]
    for o in range(1, n):
        stat_copy(o).wait_recv()
        total = total + stats_in[o]
    one, two, count = total[0:1], total[1:2], total[2:3]
    kurt_out[...] = (count + 1.0) / (count - 1.0) * (count * two / (one * one) - 1.0)
    for o in range(1, n):
        stat_copy(o).wait_send()

    @pl.loop(0, STEPS)
    def _(q):
        exchange(q).wait_send()

        @pl.when(chip < last)
        def _():
            onward(q, me + 2).wait_send()

        @pl.when(chip == last)
        def _():
            @pl.when(q // per_slab < last)
            def _():
                dump_send(q).wait_send()

            @pl.when(q // per_slab == last)
            def _():
                dump_keep(q).wait()

        hand_over(q, second, 0).wait_send()
        hand_over(q, second, 0).wait_recv()
        keep_own(q, first).wait()

    @pl.when(chip < last)
    def _():
        @pl.loop(0, per_slab)
        def _(q):
            dump_send(q).wait_recv()


def chain(gram, stats, n):
    signals = gram.shape[0]
    rows = signals // n
    half = (signals // 2, signals)
    per_slab = rows * STEPS // (signals // 2)
    dma = pltpu.SemaphoreType.DMA
    vmem = pl.BlockSpec(memory_space=pltpu.VMEM)
    hbm = pl.BlockSpec(memory_space=pl.ANY)
    return pl.pallas_call(
        functools.partial(chain_kernel, n),
        out_shape=[
            jax.ShapeDtypeStruct((signals, signals), jnp.float32),
            jax.ShapeDtypeStruct((rows, signals), jnp.float32),
            jax.ShapeDtypeStruct((1, rows), jnp.float32),
        ],
        in_specs=[vmem, vmem],
        out_specs=[hbm, hbm, vmem],
        scratch_shapes=[
            pltpu.VMEM(half, jnp.float32),
            pltpu.VMEM(half, jnp.float32),
            pltpu.VMEM(half, jnp.float32),
            pltpu.VMEM(half, jnp.float32),
            pltpu.VMEM(stats.shape, jnp.float32),
            dma((STEPS,)), dma((STEPS,)), dma((STEPS,)), dma((STEPS,)),
            dma((STEPS,)), dma((STEPS,)), dma((STEPS,)), dma((STEPS,)), dma((per_slab,)),
            dma((n,)), dma((n,)),
        ],
        compiler_params=pltpu.CompilerParams(collective_id=0, has_side_effects=True),
    )(gram, stats)


def per_device(voltages, antenna_flags, channel_flags):
    n = lax.axis_size("tm")
    local_volts = voltages[0]
    _, signals, samples = local_volts.shape
    intervals = antenna_flags.shape[1]
    segment_length = samples // intervals
    total_samples = samples * n
    keep_weight = channel_flags[0][:, None] * antenna_flags[0]
    keep_weight = jnp.swapaxes(keep_weight, 0, 1)
    shaped = local_volts.reshape(2, signals, intervals, segment_length)
    masked = (shaped * keep_weight[None, :, :, None].astype(jnp.bfloat16)).reshape(
        2, signals, samples
    )
    real_part = jnp.einsum("rst,rut->su", masked, masked, preferred_element_type=jnp.float32)
    cross_term = jnp.einsum("st,ut->su", masked[1], masked[0], preferred_element_type=jnp.float32)
    imag_part = cross_term - jnp.swapaxes(cross_term, 0, 1)
    row_ids = jnp.arange(signals, dtype=jnp.int32)
    upper_half = row_ids[:, None] <= row_ids[None, :]
    gram_block = jnp.where(upper_half, real_part, imag_part) / total_samples
    real_volts = masked[0].astype(jnp.float32)
    imag_volts = masked[1].astype(jnp.float32)
    energy = real_volts * real_volts + imag_volts * imag_volts
    moment_one = jnp.sum(energy, axis=-1)
    moment_two = jnp.sum(energy * energy, axis=-1)
    valid_count = jnp.sum(keep_weight.astype(jnp.float32), axis=-1) * segment_length
    stats = jnp.stack([moment_one, moment_two, valid_count]).reshape(3, n, signals // n)
    stats = jnp.pad(jnp.swapaxes(stats, 0, 1), ((0, 0), (0, 5), (0, 0)))
    running, dump_rows, kurtosis = chain(gram_block, stats, n)
    return (running[None, None], dump_rows[None], kurtosis)


def solution(mesh):
    return jax.shard_map(
        per_device,
        mesh=mesh,
        in_specs=(P("band", None, None, "tm"), P("band", "tm", None), P("band", "tm")),
        out_specs=(P("band", "tm", None, None), P("band", "tm", None), P("band", "tm")),
        check_vma=False,
    )
```

time: 304 us -> 140 us (0.46)
  waiting for transfers between devices: 133 us -> 0 us
  Pallas kernels: 0 us -> 63.9 us
  other arithmetic: 67.4 us -> 8.75 us
  blocking collectives: 22.9 us -> 0 us
  between operations: 14.1 us -> 0.7 us
    all_gather x1 -> x0, waiting for transfers between devices: 132 us -> none  [prefix(): gathered = lax.all_gather(part, axis)]
    pallas_call x0 -> x1, Pallas kernels: none -> 63.9 us  [chain(): pl.pallas_call(functools.partial(chain_kernel, n), out_shape=[jax.ShapeDt...]
    add x7 -> x0, other arithmetic: 49.6 us -> none  [add_terms(): return jax.tree.map(jnp.add, earlier, later)]
    psum x1 -> x0, blocking collectives: 22.9 us -> none  [per_device(): lax.psum((moment_one, moment_two, valid_count), 'tm')]
    broadcast_in_dim x2 -> x0, other arithmetic: 7.55 us -> none  [per_device(): return (running[None, None], dump_rows[None], kurtosis[None])]
    unnamed x8 -> x9, local copies, waits for them, and re-layouts: 18.4 us -> 21.4 us
  transfers between devices with their start and end apart: 2 -> 0, of which waited for: 1 -> 0; matrix products, arithmetic and copies ran while one was open for 21% -> 0% of each run, Pallas kernels for 0% -> 0%
where the time goes in v1:
time: 140 us
  Pallas kernels  63.9 us (46%)
  local copies, waits for them, and re-layouts  40.4 us (29%)
  matrix products  25.8 us (18%)
  other arithmetic  8.75 us (6%)
    pallas_call x1, Pallas kernels, chain(): pl.pallas_call(functools.partial(chain_kernel, n), out_shape=[jax.ShapeDt...  63.9 us
    unnamed x9, local copies, waits for them, and re-layouts  21.4 us
    dot_general x1, matrix products, per_device(): jnp.einsum('rst,rut->su', masked, masked, preferred_element_type=jnp.floa...  19.8 us
    another operation x1, local copies, waits for them, and re-layouts, per_device(): shaped = local_volts.reshape(2, signals, intervals, segment_length)  11.6 us
    dot_general x1, matrix products, per_device(): jnp.einsum('st,ut->su', masked[1], masked[0], preferred_element_type=jnp....  6.07 us
    dot_general x1, local copies, waits for them, and re-layouts, per_device(): jnp.einsum('st,ut->su', masked[1], masked[0], preferred_element_type=jnp....  5.35 us
    mul x1, other arithmetic, per_device(): shaped * keep_weight[None, :, :, None].astype(jnp.bfloat16)  4.67 us

profile of v1, /device:TPU:31, one launch (start us, length us, event | category | flops | bytes accessed | tf_op | source)
XLA Modules:
  0.0 139.6 jit_solution(6194634123522283769)
XLA Ops:
  0.6 0.8 convert_reduce_fusion
  1.5 0.8 fusion.20
  2.3 0.2 copy.8
  2.5 1.2 mul.62
  3.8 3.4 %copy.12 = bf16[128,8,8,256]{3,1,2,0:T(8,128)(2,1)} copy(bf16[128,8,8,256]{3,2,1,0:T(8,128)(2,1)S(1)} %bitcast.47) | data formatting | bytes 8388608
  7.1 11.8 %copy.9 = bf16[1,2,1024,2048]{2,3,1,0:T(8,128)(2,1)} copy(bf16[1,2,1024,2048]{3,2,1,0:T(8,128)(2,1)} %param.3) | data formatting | bytes 16777216 | tf_op args[0]
  19.0 11.6 %copy.10 = bf16[2,1024,8,256]{3,1,2,0:T(8,128)(2,1)} copy(bf16[2,1024,8,256]{1,3,2,0:T(8,128)(2,1)} %bitcast.46) | data formatting | bytes 16777216 | tf_op jit(solution)/shard_map/reshape;squeeze | solution.py:202
  30.6 4.7 %broadcast_multiply_fusion = bf16[2,1024,8,256]{3,1,2,0:T(8,128)(2,1)S(1)} fusion(bf16[2,1024,8,256]{3,1,2,0:T(8,128)(2,1)} %copy.10, bf16[1024,8]{0,1:T(8,128)(2,1)S(1)} %fusion.20), kind=kLoop, calls=%fused_computation.12 | loop fusion | flops 4194304 | bytes 16793600 | tf_op jit(solution)/shard_map/mul | solution.py:203
  35.3 2.4 %fusion.3 = (f32[1024]{0:T(1024)S(1)}, f32[1024]{0:T(1024)S(1)}) fusion(bf16[2,1024,8,256]{3,1,2,0:T(8,128)(2,1)S(1)} %broadcast_multiply_fusion), kind=kLoop, calls=%fused_computation.5 | loop fusion | flops 16775168 | bytes 8396800 | tf_op jit(solution)/shard_map/reduce_sum | solution.py:215
  37.7 6.1 %fusion.14 = f32[1024,1024]{1,0:T(8,128)} fusion(bf16[2,1024,8,256]{3,1,2,0:T(8,128)(2,1)S(1)} %broadcast_multiply_fusion), kind=kOutput, calls=%fused_computation.17 | convolution fusion | flops 4294967296 | bytes 12582912 | tf_op jit(solution)/shard_map/st,ut->su/dot_general | solution.py:207
  43.8 0.6 pad.4.stats
  44.4 5.3 %copy.11 = f32[1024,1024]{0,1:T(8,128)} copy(f32[1024,1024]{1,0:T(8,128)} %fusion.14) | data formatting | bytes 8388608 | tf_op jit(solution)/shard_map/st,ut->su/dot_general | solution.py:207
  49.7 19.8 %fusion.5.gram = f32[1024,1024]{1,0:T(8,128)} fusion(f32[1024,1024]{1,0:T(8,128)} %fusion.14, f32[1024,1024]{0,1:T(8,128)} %copy.11, bf16[1,2,1024,2048]{3,2,1,0:T(8,128)(2,1)} %param.3, bf16[1024,2048]{1,0:T(8,128)(2,1)} %bitcast.48), kind=kOutput, calls=%fused_computation.8 | convolution fusion | flops 8598323200 | bytes 25165824 | tf_op jit(solution)/shard_map/rst,rut->su/dot_general | solution.py:206
  69.5 63.9 %shard_map.58 = (f32[1024,1024]{1,0:T(8,128)}, f32[128,1024]{1,0:T(8,128)}, f32[1,128]{1,0:T(1,128)}) custom-call(f32[1024,1024]{1,0:T(8,128)} %fusion.5.gram, f32[8,8,128]{2,1,0:T(8,128)} %pad.4.stats), custom_call_target="tpu_custom_call" | custom-call | tf_op jit(solution)/shard_map/pallas_call | solution.py:170
  133.5 0.0 copy-start
  133.5 0.0 copy-start.1
  133.5 4.8 %copy.16 = f32[1,1,1024,1024]{3,2,1,0:T(8,128)} copy(f32[1,1,1024,1024]{3,2,1,0:T(8,128)} %bitcast.49) | data formatting | bytes 8388608
  138.3 0.0 copy-done
  138.3 0.8 copy.17
  139.1 0.0 copy-done.1
  139.1 0.5 copy.18
  (2 shorter events, 0.0 us)
Async XLA Ops:
  133.5 4.9 %copy-start = (f32[128,1024]{1,0:T(8,128)S(1)}, f32[128,1024]{1,0:T(8,128)}, u32[]{:S(2)}) copy-start(f32[128,1024]{1,0:T(8,128)} %get-tuple-element.7) | copy-start | bytes 1572868
  133.5 5.7 %copy-start.1 = (f32[1,128]{1,0:T(1,128)S(1)}, f32[1,128]{1,0:T(1,128)}, u32[]{:S(2)}) copy-start(f32[1,128]{1,0:T(1,128)} %get-tuple-element.16) | copy-start | bytes 1540

commit v2 on v1

--- a/solution.py
+++ b/solution.py
@@ -12,9 +12,9 @@
 
 
 def chain_kernel(
-    n, gram, stats, run_out, dump_out, kurt_out,
-    partner, earlier, first, second, stats_in,
-    x_send, x_recv, c_send, c_recv, p_send, p_recv, o_sem, d_send, d_recv, s_send, s_recv,
+    n, volts, antenna, channel, run_out, dump_out, kurt_out,
+    x, keep, gram, stats, partner, earlier, first, second, stats_in,
+    load, x_send, x_recv, c_send, c_recv, p_send, p_recv, o_sem, d_send, d_recv, s_send, s_recv,
 ):
     me = lax.axis_index("tm")
     chips = n // 2
@@ -24,6 +24,72 @@
     step_rows = chips * rows // STEPS
     per_slab = rows // step_rows
     last = chips - 1
+    _, signals, samples = x.shape
+    intervals = antenna.shape[0]
+    length = samples // intervals
+    pair = 2 * rows
+    block = stats.shape[2]
+    blocks = signals // block
+    share = block // rows
+    early = per_slab // 2
+    pieces = chips // early
+
+    def fetch(b):
+        part = (slice(None), pl.ds(pl.multiple_of(b * block, block), block))
+        return pltpu.make_async_copy(volts.at[part], x.at[part], load.at[b])
+
+    def mask_block(b):
+        here = pl.ds(pl.multiple_of(b * block, block), block)
+        columns = jnp.transpose(keep[:, here])
+        for i in range(intervals):
+            times = pl.ds(i * length, length)
+            weight = jnp.broadcast_to(columns[:, i : i + 1], (block, length)).astype(x.dtype)
+            for part in range(2):
+                x[part, here, times] = x[part, here, times] * weight
+
+    def product(a, a_rows, b, b_rows):
+        return lax.dot_general(
+            x[a, a_rows], x[b, b_rows], (((1,), (1,)), ((), ())),
+            preferred_element_type=jnp.float32)
+
+    def gram_piece(r, c):
+        left = pl.ds(pl.multiple_of(r * pair, pair), pair)
+        right = pl.ds(pl.multiple_of(c * pair, pair), pair)
+        scale = 1.0 / (samples * n)
+
+        def real():
+            return (product(0, left, 0, right) + product(1, left, 1, right)) * scale
+
+        def imag():
+            return (product(1, left, 0, right) - product(0, left, 1, right)) * scale
+
+        @pl.when(c > r)
+        def _():
+            gram[left, right] = real()
+
+        @pl.when(c < r)
+        def _():
+            gram[left, right] = imag()
+
+        @pl.when(c == r)
+        def _():
+            row = lax.broadcasted_iota(jnp.int32, (pair, pair), 0)
+            column = lax.broadcasted_iota(jnp.int32, (pair, pair), 1)
+            gram[left, right] = jnp.where(row <= column, real(), imag())
+
+    def moments(b):
+        here = pl.ds(pl.multiple_of(b * block, block), block)
+        one = jnp.zeros((block, 128), jnp.float32)
+        two = jnp.zeros((block, 128), jnp.float32)
+        for t in range(samples // 128):
+            real = x[0, here, pl.ds(t * 128, 128)].astype(jnp.float32)
+            imag = x[1, here, pl.ds(t * 128, 128)].astype(jnp.float32)
+            energy = real * real + imag * imag
+            one = one + energy
+            two = two + energy * energy
+        stats[b, 0:1] = jnp.sum(jnp.transpose(one), axis=0, keepdims=True)
+        stats[b, 1:2] = jnp.sum(jnp.transpose(two), axis=0, keepdims=True)
+        stats[b, 2:3] = jnp.sum(keep[:, here], axis=0, keepdims=True) * length
 
     def at(q, parity):
         slab, part = q // per_slab, q % per_slab
@@ -64,20 +130,34 @@
     def stat_copy(o):
         to = lax.rem(me + o, n)
         return pltpu.make_async_remote_copy(
-            stats.at[to], stats_in.at[o], s_send.at[o], s_recv.at[o],
+            stats.at[to // share], stats_in.at[o], s_send.at[o], s_recv.at[o],
             device_id={"tm": to}, device_id_type=MESH)
 
     barrier = pltpu.get_barrier_semaphore()
     for o in range(1, n):
         pl.semaphore_signal(barrier, inc=1, device_id={"tm": lax.rem(me + o, n)}, device_id_type=MESH)
+
+    @pl.loop(0, blocks)
+    def _(b):
+        fetch(b).start()
+
+    keep[...] = (antenna[...] * channel[...]).astype(jnp.float32)
+    stats[...] = jnp.zeros_like(stats)
+
+    @pl.loop(0, blocks)
+    def _(b):
+        fetch(b).wait()
+        mask_block(b)
+
+    @pl.loop(0, chips)
+    def _(c):
+        gram_piece(0, c)
+
     pl.semaphore_wait(barrier, n - 1)
 
-    @pl.loop(0, STEPS)
+    @pl.loop(0, per_slab)
     def _(q):
         exchange(q).start()
-
-    for o in range(1, n):
-        stat_copy(o).start()
 
     @pl.loop(0, STEPS)
     def _(q):
@@ -121,10 +201,39 @@
             hand_over(q, first, 1).start()
             keep_own(q, second).start()
 
-    total = stats[me]
+        slab, part = q // per_slab, q % per_slab
+
+        @pl.when((slab < last) & (part < early))
+        def _():
+            @pl.loop(0, pieces)
+            def _(c):
+                gram_piece(slab + 1, part * pieces + c)
+
+            @pl.when(part == early - 1)
+            def _():
+                @pl.loop(0, per_slab)
+                def _(k):
+                    exchange((slab + 1) * per_slab + k).start()
+
+        turn = slab * early + part - early
+
+        @pl.when((part >= early) & (turn < blocks))
+        def _():
+            moments(turn)
+
+            @pl.when(turn == blocks - 1)
+            def _():
+                for o in range(1, n):
+                    stat_copy(o).start()
+
+    total = stats[me // share]
     for o in range(1, n):
         stat_copy(o).wait_recv()
         total = total + stats_in[o]
+    mine = total[:, 0:rows]
+    for k in range(1, share):
+        mine = jnp.where(me % share == k, total[:, k * rows : (k + 1) * rows], mine)
+    total = mine
     one, two, count = total[0:1], total[1:2], total[2:3]
     kurt_out[...] = (count + 1.0) / (count - 1.0) * (count * two / (one * one) - 1.0)
     for o in range(1, n):
@@ -159,9 +268,11 @@
             dump_send(q).wait_recv()
 
 
-def chain(gram, stats, n):
-    signals = gram.shape[0]
+def chain(volts, antenna, channel, n):
+    _, signals, samples = volts.shape
+    intervals = antenna.shape[0]
     rows = signals // n
+    block = max(rows, 128)
     half = (signals // 2, signals)
     per_slab = rows * STEPS // (signals // 2)
     dma = pltpu.SemaphoreType.DMA
@@ -174,50 +285,32 @@
             jax.ShapeDtypeStruct((rows, signals), jnp.float32),
             jax.ShapeDtypeStruct((1, rows), jnp.float32),
         ],
-        in_specs=[vmem, vmem],
+        in_specs=[hbm, vmem, vmem],
         out_specs=[hbm, hbm, vmem],
         scratch_shapes=[
+            pltpu.VMEM(volts.shape, volts.dtype),
+            pltpu.VMEM((intervals, signals), jnp.float32),
+            pltpu.VMEM((signals, signals), jnp.float32),
+            pltpu.VMEM((signals // block, 8, block), jnp.float32),
             pltpu.VMEM(half, jnp.float32),
             pltpu.VMEM(half, jnp.float32),
             pltpu.VMEM(half, jnp.float32),
             pltpu.VMEM(half, jnp.float32),
-            pltpu.VMEM(stats.shape, jnp.float32),
+            pltpu.VMEM((n, 8, block), jnp.float32),
+            dma((signals // block,)),
             dma((STEPS,)), dma((STEPS,)), dma((STEPS,)), dma((STEPS,)),
             dma((STEPS,)), dma((STEPS,)), dma((STEPS,)), dma((STEPS,)), dma((per_slab,)),
             dma((n,)), dma((n,)),
         ],
         compiler_params=pltpu.CompilerParams(collective_id=0, has_side_effects=True),
-    )(gram, stats)
+    )(volts, antenna, channel)
 
 
 def per_device(voltages, antenna_flags, channel_flags):
     n = lax.axis_size("tm")
-    local_volts = voltages[0]
-    _, signals, samples = local_volts.shape
-    intervals = antenna_flags.shape[1]
-    segment_length = samples // intervals
-    total_samples = samples * n
-    keep_weight = channel_flags[0][:, None] * antenna_flags[0]
-    keep_weight = jnp.swapaxes(keep_weight, 0, 1)
-    shaped = local_volts.reshape(2, signals, intervals, segment_length)
-    masked = (shaped * keep_weight[None, :, :, None].astype(jnp.bfloat16)).reshape(
-        2, signals, samples
+    running, dump_rows, kurtosis = chain(
+        voltages[0], antenna_flags[0], channel_flags[0][:, None], n
     )
-    real_part = jnp.einsum("rst,rut->su", masked, masked, preferred_element_type=jnp.float32)
-    cross_term = jnp.einsum("st,ut->su", masked[1], masked[0], preferred_element_type=jnp.float32)
-    imag_part = cross_term - jnp.swapaxes(cross_term, 0, 1)
-    row_ids = jnp.arange(signals, dtype=jnp.int32)
-    upper_half = row_ids[:, None] <= row_ids[None, :]
-    gram_block = jnp.where(upper_half, real_part, imag_part) / total_samples
-    real_volts = masked[0].astype(jnp.float32)
-    imag_volts = masked[1].astype(jnp.float32)
-    energy = real_volts * real_volts + imag_volts * imag_volts
-    moment_one = jnp.sum(energy, axis=-1)
-    moment_two = jnp.sum(energy * energy, axis=-1)
-    valid_count = jnp.sum(keep_weight.astype(jnp.float32), axis=-1) * segment_length
-    stats = jnp.stack([moment_one, moment_two, valid_count]).reshape(3, n, signals // n)
-    stats = jnp.pad(jnp.swapaxes(stats, 0, 1), ((0, 0), (0, 5), (0, 0)))
-    running, dump_rows, kurtosis = chain(gram_block, stats, n)
     return (running[None, None], dump_rows[None], kurtosis)
 
 

time: 140 us -> 75.8 us (0.54)
  local copies, waits for them, and re-layouts: 40.4 us -> 7.48 us
  matrix products: 25.8 us -> 0 us
  other arithmetic: 8.75 us -> 0 us
  Pallas kernels: 63.9 us -> 67.5 us
    dot_general x2 -> x0, matrix products: 25.8 us -> none  [the longest x1 19.8 us: per_device(): jnp.einsum('rst,rut->su', masked, masked, preferred_element_type=jnp.floa...]
    unnamed x9 -> x7, local copies, waits for them, and re-layouts: 21.4 us -> 6.16 us
    another operation x1, local copies, waits for them, and re-layouts: 11.6 us -> 1.32 us  [per_device(): channel_flags[0][:, None]]
    dot_general x1 -> x0, local copies, waits for them, and re-layouts: 5.35 us -> none  [per_device(): jnp.einsum('st,ut->su', masked[1], masked[0], preferred_element_type=jnp....]
    mul x2 -> x0, other arithmetic: 4.67 us -> none  [the longest x1 4.67 us: per_device(): shaped * keep_weight[None, :, :, None].astype(jnp.bfloat16)]
    pallas_call x1, Pallas kernels: 63.9 us -> 67.5 us  [chain(): pl.pallas_call(functools.partial(chain_kernel, n), out_shape=[jax.ShapeDt...]
    reduce_sum x2 -> x0, other arithmetic: 3.22 us -> none  [the longest x1 2.38 us: per_device(): moment_one = jnp.sum(energy, axis=-1)]
where the time goes in v2:
time: 75.8 us; the launch traced here: 75.6 us
  Pallas kernels  67.5 us (89%)
  local copies, waits for them, and re-layouts  7.48 us (10%)
    pallas_call x1, Pallas kernels, chain(): pl.pallas_call(functools.partial(chain_kernel, n), out_shape=[jax.ShapeDt...  67.5 us
    unnamed x7, local copies, waits for them, and re-layouts  6.16 us

profile of v2, /device:TPU:31, one launch (start us, length us, event | category | flops | bytes accessed | tf_op | source)
XLA Modules:
  0.0 75.6 jit_solution(6895336382990614269)
XLA Ops:
  0.6 1.3 %copy.6.channel = s32[8,1]{1,0:T(8,128)} copy(s32[8,1]{0,1:T(1,128)} %bitcast.9) | data formatting | bytes 64 | tf_op jit(solution)/shard_map/broadcast_in_dim;squeeze | solution.py:312
  2.0 67.5 %shard_map.58 = (f32[1024,1024]{1,0:T(8,128)}, f32[128,1024]{1,0:T(8,128)}, f32[1,128]{1,0:T(1,128)}) custom-call(bf16[2,1024,2048]{2,1,0:T(8,128)(2,1)} %bitcast.5, s32[8,1024]{1,0:T(8,128)} %bitcast.8, s32[8,1]{1,0:T(8,128)} %copy.6.channel), custom_call_target="tpu_custom_call" | custom-call | tf_op jit(solution)/shard_map/pallas_call | solution.py:281
  69.5 0.0 copy-start
  69.5 0.0 copy-start.1
  69.5 4.8 %copy.10 = f32[1,1,1024,1024]{3,2,1,0:T(8,128)} copy(f32[1,1,1024,1024]{3,2,1,0:T(8,128)} %bitcast.6) | data formatting | bytes 8388608
  74.3 0.0 copy-done
  74.3 0.8 %copy.11 = f32[1,128,1024]{2,1,0:T(8,128)} copy(f32[1,128,1024]{2,1,0:T(8,128)S(1)} %bitcast.7) | data formatting | bytes 1048576
  75.1 0.0 copy-done.1
  75.1 0.5 copy.12
Async XLA Ops:
  69.5 4.9 %copy-start = (f32[128,1024]{1,0:T(8,128)S(1)}, f32[128,1024]{1,0:T(8,128)}, u32[]{:S(2)}) copy-start(f32[128,1024]{1,0:T(8,128)} %get-tuple-element.7) | copy-start | bytes 1572868
  69.5 5.7 %copy-start.1 = (f32[1,128]{1,0:T(1,128)S(1)}, f32[1,128]{1,0:T(1,128)}, u32[]{:S(2)}) copy-start(f32[1,128]{1,0:T(1,128)} %get-tuple-element.14) | copy-start | bytes 1540

commit v3 on v2

--- a/solution.py
+++ b/solution.py
@@ -9,6 +9,7 @@
 
 MESH = pl.DeviceIdType.MESH
 STEPS = 32
+VMEM_BYTES = 57 * 2**20
 
 
 def chain_kernel(
@@ -21,8 +22,8 @@
     chip, core = me // 2, me % 2
     other = chip * 2 + (1 - core)
     rows = gram.shape[0] // n
-    step_rows = chips * rows // STEPS
-    per_slab = rows // step_rows
+    per_slab = STEPS // chips
+    width = gram.shape[0] // per_slab
     last = chips - 1
     _, signals, samples = x.shape
     intervals = antenna.shape[0]
@@ -31,8 +32,10 @@
     block = stats.shape[2]
     blocks = signals // block
     share = block // rows
-    early = per_slab // 2
-    pieces = chips // early
+    wide = max(pair, width)
+    pieces = signals // wide
+    steps = chips * pieces
+    chunks = wide // width
 
     def fetch(b):
         part = (slice(None), pl.ds(pl.multiple_of(b * block, block), block))
@@ -40,10 +43,10 @@
 
     def mask_block(b):
         here = pl.ds(pl.multiple_of(b * block, block), block)
-        columns = jnp.transpose(keep[:, here])
+        kept = jnp.transpose(keep[:, here])
         for i in range(intervals):
             times = pl.ds(i * length, length)
-            weight = jnp.broadcast_to(columns[:, i : i + 1], (block, length)).astype(x.dtype)
+            weight = jnp.broadcast_to(kept[:, i : i + 1], (block, length)).astype(x.dtype)
             for part in range(2):
                 x[part, here, times] = x[part, here, times] * weight
 
@@ -54,7 +57,7 @@
 
     def gram_piece(r, c):
         left = pl.ds(pl.multiple_of(r * pair, pair), pair)
-        right = pl.ds(pl.multiple_of(c * pair, pair), pair)
+        right = pl.ds(pl.multiple_of(c * wide, wide), wide)
         scale = 1.0 / (samples * n)
 
         def real():
@@ -63,18 +66,21 @@
         def imag():
             return (product(1, left, 0, right) - product(0, left, 1, right)) * scale
 
-        @pl.when(c > r)
+        above = c * wide >= (r + 1) * pair
+        below = (c + 1) * wide <= r * pair
+
+        @pl.when(above)
         def _():
             gram[left, right] = real()
 
-        @pl.when(c < r)
+        @pl.when(below)
         def _():
             gram[left, right] = imag()
 
-        @pl.when(c == r)
-        def _():
-            row = lax.broadcasted_iota(jnp.int32, (pair, pair), 0)
-            column = lax.broadcasted_iota(jnp.int32, (pair, pair), 1)
+        @pl.when(jnp.logical_not(above | below))
+        def _():
+            row = lax.broadcasted_iota(jnp.int32, (pair, wide), 0) + r * pair
+            column = lax.broadcasted_iota(jnp.int32, (pair, wide), 1) + c * wide
             gram[left, right] = jnp.where(row <= column, real(), imag())
 
     def moments(b):
@@ -91,41 +97,38 @@
         stats[b, 1:2] = jnp.sum(jnp.transpose(two), axis=0, keepdims=True)
         stats[b, 2:3] = jnp.sum(keep[:, here], axis=0, keepdims=True) * length
 
+    def columns(q):
+        return pl.ds(pl.multiple_of((q % per_slab) * width, width), width)
+
     def at(q, parity):
-        slab, part = q // per_slab, q % per_slab
-        return pl.ds(pl.multiple_of((slab * 2 + parity) * rows + part * step_rows, 8), step_rows)
-
-    def flat(q):
-        return pl.ds(pl.multiple_of(q * step_rows, 8), step_rows)
+        first_row = ((q // per_slab) * 2 + parity) * rows
+        return (pl.ds(pl.multiple_of(first_row, rows), rows), columns(q))
 
     def exchange(q):
         return pltpu.make_async_remote_copy(
-            gram.at[at(q, 1 - core)], partner.at[flat(q)], x_send.at[q], x_recv.at[q],
+            gram.at[at(q, 1 - core)], partner.at[q], x_send.at[q], x_recv.at[q],
             device_id={"tm": other}, device_id_type=MESH)
 
     def onward(q, to):
         return pltpu.make_async_remote_copy(
-            second.at[flat(q)], earlier.at[flat(q)], c_send.at[q], c_recv.at[q],
+            second.at[q], earlier.at[q], c_send.at[q], c_recv.at[q],
             device_id={"tm": to}, device_id_type=MESH)
 
     def hand_over(q, source, parity):
         return pltpu.make_async_remote_copy(
-            source.at[flat(q)], run_out.at[at(q, parity)], p_send.at[q], p_recv.at[q],
+            source.at[q], run_out.at[at(q, parity)], p_send.at[q], p_recv.at[q],
             device_id={"tm": other}, device_id_type=MESH)
 
     def keep_own(q, source):
-        return pltpu.make_async_copy(source.at[flat(q)], run_out.at[at(q, core)], o_sem.at[q])
-
-    def dump_rows(q):
-        return pl.ds(pl.multiple_of((q % per_slab) * step_rows, 8), step_rows)
+        return pltpu.make_async_copy(source.at[q], run_out.at[at(q, core)], o_sem.at[q])
 
     def dump_send(q):
         return pltpu.make_async_remote_copy(
-            second.at[flat(q)], dump_out.at[dump_rows(q)], d_send.at[q], d_recv.at[q % per_slab],
+            second.at[q], dump_out.at[:, columns(q)], d_send.at[q], d_recv.at[q % per_slab],
             device_id={"tm": (q // per_slab) * 2 + core}, device_id_type=MESH)
 
     def dump_keep(q):
-        return pltpu.make_async_copy(second.at[flat(q)], dump_out.at[dump_rows(q)], d_send.at[q])
+        return pltpu.make_async_copy(second.at[q], dump_out.at[:, columns(q)], d_send.at[q])
 
     def stat_copy(o):
         to = lax.rem(me + o, n)
@@ -141,41 +144,28 @@
     def _(b):
         fetch(b).start()
 
-    keep[...] = (antenna[...] * channel[...]).astype(jnp.float32)
+    for i in range(intervals):
+        keep[i : i + 1] = (antenna[i : i + 1] * channel[0, i]).astype(jnp.float32)
     stats[...] = jnp.zeros_like(stats)
 
-    @pl.loop(0, blocks)
-    def _(b):
-        fetch(b).wait()
-        mask_block(b)
-
-    @pl.loop(0, chips)
-    def _(c):
-        gram_piece(0, c)
-
     pl.semaphore_wait(barrier, n - 1)
 
-    @pl.loop(0, per_slab)
-    def _(q):
-        exchange(q).start()
-
-    @pl.loop(0, STEPS)
-    def _(q):
+    def advance(q):
         exchange(q).wait_recv()
         mine = gram[at(q, core)]
-        theirs = partner[flat(q)]
+        theirs = partner[q]
         low = jnp.where(core == 0, mine, theirs)
 
         @pl.when(chip > 0)
         def _():
             onward(q, me).wait_recv()
-            first[flat(q)] = earlier[flat(q)] + low
+            first[q] = earlier[q] + low
 
         @pl.when(chip == 0)
         def _():
-            first[flat(q)] = low
-
-        second[flat(q)] = first[flat(q)] + jnp.where(core == 0, theirs, mine)
+            first[q] = low
+
+        second[q] = first[q] + jnp.where(core == 0, theirs, mine)
 
         @pl.when(chip < last)
         def _():
@@ -201,23 +191,29 @@
             hand_over(q, first, 1).start()
             keep_own(q, second).start()
 
-        slab, part = q // per_slab, q % per_slab
-
-        @pl.when((slab < last) & (part < early))
-        def _():
-            @pl.loop(0, pieces)
-            def _(c):
-                gram_piece(slab + 1, part * pieces + c)
-
-            @pl.when(part == early - 1)
-            def _():
-                @pl.loop(0, per_slab)
-                def _(k):
-                    exchange((slab + 1) * per_slab + k).start()
-
-        turn = slab * early + part - early
-
-        @pl.when((part >= early) & (turn < blocks))
+    @pl.loop(0, steps + 1)
+    def _(g):
+        @pl.when(g < pieces)
+        def _():
+            for k in range(wide // block):
+                fetch(g * (wide // block) + k).wait()
+                mask_block(g * (wide // block) + k)
+
+        @pl.when(g < steps)
+        def _():
+            gram_piece(g // pieces, g % pieces)
+            for k in range(chunks):
+                exchange(g * chunks + k).start()
+
+        @pl.when(g > 0)
+        def _():
+            @pl.loop(0, chunks)
+            def _(k):
+                advance((g - 1) * chunks + k)
+
+        turn = g - pieces
+
+        @pl.when((turn >= 0) & (turn < blocks))
         def _():
             moments(turn)
 
@@ -273,8 +269,8 @@
     intervals = antenna.shape[0]
     rows = signals // n
     block = max(rows, 128)
-    half = (signals // 2, signals)
-    per_slab = rows * STEPS // (signals // 2)
+    per_slab = STEPS // (n // 2)
+    half = (STEPS, rows, signals // per_slab)
     dma = pltpu.SemaphoreType.DMA
     vmem = pl.BlockSpec(memory_space=pltpu.VMEM)
     hbm = pl.BlockSpec(memory_space=pl.ANY)
@@ -285,7 +281,11 @@
             jax.ShapeDtypeStruct((rows, signals), jnp.float32),
             jax.ShapeDtypeStruct((1, rows), jnp.float32),
         ],
-        in_specs=[hbm, vmem, vmem],
+        in_specs=[
+            pl.BlockSpec(memory_space=pltpu.HBM),
+            vmem,
+            pl.BlockSpec(memory_space=pltpu.SMEM),
+        ],
         out_specs=[hbm, hbm, vmem],
         scratch_shapes=[
             pltpu.VMEM(volts.shape, volts.dtype),
@@ -302,14 +302,16 @@
             dma((STEPS,)), dma((STEPS,)), dma((STEPS,)), dma((STEPS,)), dma((per_slab,)),
             dma((n,)), dma((n,)),
         ],
-        compiler_params=pltpu.CompilerParams(collective_id=0, has_side_effects=True),
+        compiler_params=pltpu.CompilerParams(
+            collective_id=0, has_side_effects=True, vmem_limit_bytes=VMEM_BYTES
+        ),
     )(volts, antenna, channel)
 
 
 def per_device(voltages, antenna_flags, channel_flags):
     n = lax.axis_size("tm")
     running, dump_rows, kurtosis = chain(
-        voltages[0], antenna_flags[0], channel_flags[0][:, None], n
+        voltages[0], antenna_flags[0], channel_flags, n
     )
     return (running[None, None], dump_rows[None], kurtosis)
 

time: 75.8 us -> 72.5 us (0.956)
  Pallas kernels: 67.5 us -> 65.5 us
  local copies, waits for them, and re-layouts: 7.48 us -> 6.16 us
    pallas_call x1, Pallas kernels: 67.5 us -> 65.5 us  [chain(): pl.pallas_call(functools.partial(chain_kernel, n), out_shape=[jax.ShapeDt...]
    another operation x1 -> x0, local copies, waits for them, and re-layouts: 1.32 us -> none  [per_device(): channel_flags[0][:, None]]
where the time goes in v3:
time: 72.5 us; the launch traced here: 72.3 us
  Pallas kernels  65.5 us (90%)
  local copies, waits for them, and re-layouts  6.16 us (8%)
    pallas_call x1, Pallas kernels, chain(): pl.pallas_call(functools.partial(chain_kernel, n), out_shape=[jax.ShapeDt...  65.5 us
    unnamed x7, local copies, waits for them, and re-layouts  6.16 us

profile of v3, /device:TPU:31, one launch (start us, length us, event | category | flops | bytes accessed | tf_op | source)
XLA Modules:
  0.0 72.3 jit_solution(1716479285079570894)
XLA Ops:
  0.6 65.5 %shard_map.58 = (f32[1024,1024]{1,0:T(8,128)}, f32[128,1024]{1,0:T(8,128)}, f32[1,128]{1,0:T(1,128)}) custom-call(bf16[2,1024,2048]{2,1,0:T(8,128)(2,1)} %bitcast.4, s32[8,1024]{1,0:T(8,128)} %bitcast.7, s32[1,8]{1,0:T(1,128)} %channel.1), custom_call_target="tpu_custom_call" | custom-call | tf_op jit(solution)/shard_map/pallas_call | solution.py:277
  66.1 0.0 copy-start
  66.1 0.0 copy-start.1
  66.1 4.8 %copy.9 = f32[1,1,1024,1024]{3,2,1,0:T(8,128)} copy(f32[1,1,1024,1024]{3,2,1,0:T(8,128)} %bitcast.5) | data formatting | bytes 8388608
  71.0 0.0 copy-done
  71.0 0.8 %copy.10 = f32[1,128,1024]{2,1,0:T(8,128)} copy(f32[1,128,1024]{2,1,0:T(8,128)S(1)} %bitcast.6) | data formatting | bytes 1048576
  71.8 0.0 copy-done.1
  71.8 0.5 copy.11
Async XLA Ops:
  66.1 4.9 %copy-start = (f32[128,1024]{1,0:T(8,128)S(1)}, f32[128,1024]{1,0:T(8,128)}, u32[]{:S(2)}) copy-start(f32[128,1024]{1,0:T(8,128)} %get-tuple-element.7) | copy-start | bytes 1572868
  66.1 5.7 %copy-start.1 = (f32[1,128]{1,0:T(1,128)S(1)}, f32[1,128]{1,0:T(1,128)}, u32[]{:S(2)}) copy-start(f32[1,128]{1,0:T(1,128)} %get-tuple-element.14) | copy-start | bytes 1540

commit v4 on v3

--- a/solution.py
+++ b/solution.py
@@ -9,13 +9,14 @@
 
 MESH = pl.DeviceIdType.MESH
 STEPS = 32
-VMEM_BYTES = 57 * 2**20
+LAG = 3
+VMEM_BYTES = 46 * 2**20
 
 
 def chain_kernel(
     n, volts, antenna, channel, run_out, dump_out, kurt_out,
-    x, keep, gram, stats, partner, earlier, first, second, stats_in,
-    load, x_send, x_recv, c_send, c_recv, p_send, p_recv, o_sem, d_send, d_recv, s_send, s_recv,
+    x, keep, gram, stats, partner, raw, sibling, earlier, first, second, stats_in,
+    load, x_send, x_recv, r_send, r_recv, c_send, v_send, c_recv, p_send, p_recv, o_sem, d_send, d_recv, s_send, s_recv,
 ):
     me = lax.axis_index("tm")
     chips = n // 2
@@ -25,6 +26,8 @@
     per_slab = STEPS // chips
     width = gram.shape[0] // per_slab
     last = chips - 1
+    even = chip % 2 == 0
+    lag = jnp.where(even & (chip > 0), LAG, 0)
     _, signals, samples = x.shape
     intervals = antenna.shape[0]
     length = samples // intervals
@@ -109,9 +112,14 @@
             gram.at[at(q, 1 - core)], partner.at[q], x_send.at[q], x_recv.at[q],
             device_id={"tm": other}, device_id_type=MESH)
 
-    def onward(q, to):
-        return pltpu.make_async_remote_copy(
-            second.at[q], earlier.at[q], c_send.at[q], c_recv.at[q],
+    def send_raw(q, to):
+        return pltpu.make_async_remote_copy(
+            raw.at[q], sibling.at[q], r_send.at[q], r_recv.at[q],
+            device_id={"tm": to}, device_id_type=MESH)
+
+    def onward(q, to, sem):
+        return pltpu.make_async_remote_copy(
+            second.at[q], earlier.at[q], sem.at[q], c_recv.at[q],
             device_id={"tm": to}, device_id_type=MESH)
 
     def hand_over(q, source, parity):
@@ -140,36 +148,57 @@
     for o in range(1, n):
         pl.semaphore_signal(barrier, inc=1, device_id={"tm": lax.rem(me + o, n)}, device_id_type=MESH)
 
-    @pl.loop(0, blocks)
-    def _(b):
+    opening = wide // block
+    for b in range(opening):
         fetch(b).start()
 
     for i in range(intervals):
         keep[i : i + 1] = (antenna[i : i + 1] * channel[0, i]).astype(jnp.float32)
     stats[...] = jnp.zeros_like(stats)
 
+    for b in range(opening):
+        fetch(b).wait()
+
+    @pl.loop(opening, blocks)
+    def _(b):
+        fetch(b).start()
+
+    for b in range(opening):
+        mask_block(b)
+    gram_piece(0, 0)
+
     pl.semaphore_wait(barrier, n - 1)
 
+    def gather(q):
+        exchange(q).wait_recv()
+
+        @pl.when(even)
+        def _():
+            raw[q] = gram[at(q, core)] + partner[q]
+            send_raw(q, me + 2).start()
+
     def advance(q):
-        exchange(q).wait_recv()
         mine = gram[at(q, core)]
         theirs = partner[q]
         low = jnp.where(core == 0, mine, theirs)
-
-        @pl.when(chip > 0)
-        def _():
-            onward(q, me).wait_recv()
-            first[q] = earlier[q] + low
-
-        @pl.when(chip == 0)
-        def _():
-            first[q] = low
+        first[q] = low
+
+        @pl.when(chip > 1)
+        def _():
+            onward(q, me, c_send).wait_recv()
+            first[q] = first[q] + earlier[q]
+
+        @pl.when(jnp.logical_not(even))
+        def _():
+            send_raw(q, me).wait_recv()
+            first[q] = first[q] + sibling[q]
 
         second[q] = first[q] + jnp.where(core == 0, theirs, mine)
 
-        @pl.when(chip < last)
-        def _():
-            onward(q, me + 2).start()
+        @pl.when(jnp.logical_not(even) & (chip < last))
+        def _():
+            onward(q, me + 4, v_send).start()
+            onward(q, me + 2, c_send).start()
 
         @pl.when(chip == last)
         def _():
@@ -191,25 +220,36 @@
             hand_over(q, first, 1).start()
             keep_own(q, second).start()
 
-    @pl.loop(0, steps + 1)
+    @pl.loop(0, steps + 1 + LAG)
     def _(g):
-        @pl.when(g < pieces)
-        def _():
-            for k in range(wide // block):
-                fetch(g * (wide // block) + k).wait()
-                mask_block(g * (wide // block) + k)
+        @pl.when((g > 0) & (g < pieces))
+        def _():
+            for k in range(opening):
+                fetch(g * opening + k).wait()
+                mask_block(g * opening + k)
 
         @pl.when(g < steps)
         def _():
-            gram_piece(g // pieces, g % pieces)
+            @pl.when(g > 0)
+            def _():
+                gram_piece(g // pieces, g % pieces)
+
             for k in range(chunks):
                 exchange(g * chunks + k).start()
 
-        @pl.when(g > 0)
+        @pl.when((g > 0) & (g <= steps))
         def _():
             @pl.loop(0, chunks)
             def _(k):
-                advance((g - 1) * chunks + k)
+                gather((g - 1) * chunks + k)
+
+        due = g - 1 - lag
+
+        @pl.when((due >= 0) & (due < steps))
+        def _():
+            @pl.loop(0, chunks)
+            def _(k):
+                advance(due * chunks + k)
 
         turn = g - pieces
 
@@ -239,9 +279,14 @@
     def _(q):
         exchange(q).wait_send()
 
-        @pl.when(chip < last)
-        def _():
-            onward(q, me + 2).wait_send()
+        @pl.when(even)
+        def _():
+            send_raw(q, me + 2).wait_send()
+
+        @pl.when(jnp.logical_not(even) & (chip < last))
+        def _():
+            onward(q, me + 4, v_send).wait_send()
+            onward(q, me + 2, c_send).wait_send()
 
         @pl.when(chip == last)
         def _():
@@ -296,10 +341,12 @@
             pltpu.VMEM(half, jnp.float32),
             pltpu.VMEM(half, jnp.float32),
             pltpu.VMEM(half, jnp.float32),
+            pltpu.VMEM(half, jnp.float32),
+            pltpu.VMEM(half, jnp.float32),
             pltpu.VMEM((n, 8, block), jnp.float32),
             dma((signals // block,)),
             dma((STEPS,)), dma((STEPS,)), dma((STEPS,)), dma((STEPS,)),
-            dma((STEPS,)), dma((STEPS,)), dma((STEPS,)), dma((STEPS,)), dma((per_slab,)),
+            dma((STEPS,)), dma((STEPS,)), dma((STEPS,)), dma((STEPS,)), dma((STEPS,)), dma((STEPS,)), dma((STEPS,)), dma((per_slab,)),
             dma((n,)), dma((n,)),
         ],
         compiler_params=pltpu.CompilerParams(

time: 72.5 us -> 66.7 us (0.920); the launches traced: 72.3 us -> 65.5 us
  Pallas kernels: 65.5 us -> 60.2 us
  local copies, waits for them, and re-layouts: 6.16 us -> 4.72 us
    pallas_call x1, Pallas kernels: 65.5 us -> 60.2 us  [chain(): pl.pallas_call(functools.partial(chain_kernel, n), out_shape=[jax.ShapeDt...]
    unnamed x7, local copies, waits for them, and re-layouts: 6.16 us -> 4.72 us
where the time goes in v4:
time: 66.7 us; the launch traced here: 65.5 us
  Pallas kernels  60.2 us (90%)
  local copies, waits for them, and re-layouts  4.72 us (7%)
    pallas_call x1, Pallas kernels, chain(): pl.pallas_call(functools.partial(chain_kernel, n), out_shape=[jax.ShapeDt...  60.2 us
    unnamed x7, local copies, waits for them, and re-layouts  4.72 us

profile of v4, /device:TPU:31, one launch (start us, length us, event | category | flops | bytes accessed | tf_op | source)
XLA Modules:
  0.0 65.5 jit_solution(10747443719621100775)
XLA Ops:
  0.6 0.0 copy-start
  0.6 0.7 %copy-done = s32[1,8,1024]{2,1,0:T(8,128)S(1)} copy-done((s32[1,8,1024]{2,1,0:T(8,128)S(1)}, s32[1,8,1024]{2,1,0:T(8,128)}, u32[]{:S(2)}) %copy-start) | copy-done | bytes 32792
  1.4 0.0 copy-start.1
  1.4 0.7 copy-done.1
  2.0 60.2 %shard_map.58 = (f32[1024,1024]{1,0:T(8,128)S(1)}, f32[128,1024]{1,0:T(8,128)S(1)}, f32[1,128]{1,0:T(1,128)S(1)}) custom-call(bf16[2,1024,2048]{2,1,0:T(8,128)(2,1)} %bitcast.7, s32[8,1024]{1,0:T(8,128)S(1)} %bitcast.6, s32[1,8]{1,0:T(1,128)S(1)} %copy-done.1), custom_call_target="tpu_custom_call" | custom-call | tf_op jit(solution)/shard_map/pallas_call | solution.py:322
  62.2 2.0 %copy.9 = f32[1,1,1024,1024]{3,2,1,0:T(8,128)} copy(f32[1,1,1024,1024]{3,2,1,0:T(8,128)S(1)} %bitcast.4) | data formatting | bytes 8388608
  64.2 0.8 %copy.10 = f32[1,128,1024]{2,1,0:T(8,128)} copy(f32[1,128,1024]{2,1,0:T(8,128)S(1)} %bitcast.5) | data formatting | bytes 1048576
  65.0 0.5 copy.11
Async XLA Ops:
  0.6 0.8 %copy-start = (s32[1,8,1024]{2,1,0:T(8,128)S(1)}, s32[1,8,1024]{2,1,0:T(8,128)}, u32[]{:S(2)}) copy-start(s32[1,8,1024]{2,1,0:T(8,128)} %param.4) | copy-start | bytes 98308
  1.4 0.7 copy-start.1

commit v5 on v4

--- a/solution.py
+++ b/solution.py
@@ -16,7 +16,7 @@
 def chain_kernel(
     n, volts, antenna, channel, run_out, dump_out, kurt_out,
     x, keep, gram, stats, partner, raw, sibling, earlier, first, second, stats_in,
-    load, x_send, x_recv, r_send, r_recv, c_send, v_send, c_recv, p_send, p_recv, o_sem, d_send, d_recv, s_send, s_recv,
+    load, x_send, x_recv, r_send, r_recv, c_send, v_send, c_recv, p_send, p_recv, o_sem, d_send, d_recv, k_sem, s_send, s_recv,
 ):
     me = lax.axis_index("tm")
     chips = n // 2
@@ -109,34 +109,34 @@
 
     def exchange(q):
         return pltpu.make_async_remote_copy(
-            gram.at[at(q, 1 - core)], partner.at[q], x_send.at[q], x_recv.at[q],
+            gram.at[at(q, 1 - core)], partner.at[q], x_send, x_recv.at[q],
             device_id={"tm": other}, device_id_type=MESH)
 
     def send_raw(q, to):
         return pltpu.make_async_remote_copy(
-            raw.at[q], sibling.at[q], r_send.at[q], r_recv.at[q],
+            raw.at[q], sibling.at[q], r_send, r_recv.at[q],
             device_id={"tm": to}, device_id_type=MESH)
 
     def onward(q, to, sem):
         return pltpu.make_async_remote_copy(
-            second.at[q], earlier.at[q], sem.at[q], c_recv.at[q],
+            second.at[q], earlier.at[q], sem, c_recv.at[q],
             device_id={"tm": to}, device_id_type=MESH)
 
     def hand_over(q, source, parity):
         return pltpu.make_async_remote_copy(
-            source.at[q], run_out.at[at(q, parity)], p_send.at[q], p_recv.at[q],
+            source.at[q], run_out.at[at(q, parity)], p_send, p_recv,
             device_id={"tm": other}, device_id_type=MESH)
 
     def keep_own(q, source):
-        return pltpu.make_async_copy(source.at[q], run_out.at[at(q, core)], o_sem.at[q])
+        return pltpu.make_async_copy(source.at[q], run_out.at[at(q, core)], o_sem)
 
     def dump_send(q):
         return pltpu.make_async_remote_copy(
-            second.at[q], dump_out.at[:, columns(q)], d_send.at[q], d_recv.at[q % per_slab],
+            second.at[q], dump_out.at[:, columns(q)], d_send, d_recv,
             device_id={"tm": (q // per_slab) * 2 + core}, device_id_type=MESH)
 
     def dump_keep(q):
-        return pltpu.make_async_copy(second.at[q], dump_out.at[:, columns(q)], d_send.at[q])
+        return pltpu.make_async_copy(second.at[q], dump_out.at[:, columns(q)], k_sem)
 
     def stat_copy(o):
         to = lax.rem(me + o, n)
@@ -197,8 +197,8 @@
 
         @pl.when(jnp.logical_not(even) & (chip < last))
         def _():
+            onward(q, me + 2, c_send).start()
             onward(q, me + 4, v_send).start()
-            onward(q, me + 2, c_send).start()
 
         @pl.when(chip == last)
         def _():
@@ -275,38 +275,34 @@
     for o in range(1, n):
         stat_copy(o).wait_send()
 
-    @pl.loop(0, STEPS)
-    def _(q):
-        exchange(q).wait_send()
-
-        @pl.when(even)
-        def _():
-            send_raw(q, me + 2).wait_send()
-
-        @pl.when(jnp.logical_not(even) & (chip < last))
-        def _():
-            onward(q, me + 4, v_send).wait_send()
-            onward(q, me + 2, c_send).wait_send()
-
-        @pl.when(chip == last)
-        def _():
-            @pl.when(q // per_slab < last)
-            def _():
-                dump_send(q).wait_send()
-
-            @pl.when(q // per_slab == last)
-            def _():
-                dump_keep(q).wait()
-
-        hand_over(q, second, 0).wait_send()
-        hand_over(q, second, 0).wait_recv()
-        keep_own(q, first).wait()
+    def whole(count, send, recv):
+        part = pl.ds(0, count)
+        return pltpu.make_async_remote_copy(
+            second.at[part], earlier.at[part], send, recv,
+            device_id={"tm": other}, device_id_type=MESH)
+
+    whole(STEPS, x_send, p_recv).wait_send()
+    whole(STEPS, p_send, p_recv).wait()
+    pltpu.make_async_copy(second, earlier, o_sem).wait()
+
+    @pl.when(even)
+    def _():
+        whole(STEPS, r_send, p_recv).wait_send()
+
+    @pl.when(jnp.logical_not(even) & (chip < last))
+    def _():
+        whole(STEPS, c_send, p_recv).wait_send()
+        whole(STEPS, v_send, p_recv).wait_send()
+
+    @pl.when(chip == last)
+    def _():
+        whole(STEPS - per_slab, d_send, p_recv).wait_send()
+        kept = pl.ds(0, per_slab)
+        pltpu.make_async_copy(second.at[kept], earlier.at[kept], k_sem).wait()
 
     @pl.when(chip < last)
     def _():
-        @pl.loop(0, per_slab)
-        def _(q):
-            dump_send(q).wait_recv()
+        whole(per_slab, d_send, d_recv).wait_recv()
 
 
 def chain(volts, antenna, channel, n):
@@ -345,8 +341,8 @@
             pltpu.VMEM(half, jnp.float32),
             pltpu.VMEM((n, 8, block), jnp.float32),
             dma((signals // block,)),
-            dma((STEPS,)), dma((STEPS,)), dma((STEPS,)), dma((STEPS,)),
-            dma((STEPS,)), dma((STEPS,)), dma((STEPS,)), dma((STEPS,)), dma((STEPS,)), dma((STEPS,)), dma((STEPS,)), dma((per_slab,)),
+            dma, dma((STEPS,)), dma, dma((STEPS,)), dma, dma, dma((STEPS,)),
+            dma, dma, dma, dma, dma, dma,
             dma((n,)), dma((n,)),
         ],
         compiler_params=pltpu.CompilerParams(

time: 66.7 us -> 64.4 us (0.966)
  Pallas kernels: 60.2 us -> 57.9 us
    pallas_call x1, Pallas kernels: 60.2 us -> 57.9 us  [chain(): pl.pallas_call(functools.partial(chain_kernel, n), out_shape=[jax.ShapeDt...]
where the time goes in v5:
time: 64.4 us; the launch traced here: 63.3 us
  Pallas kernels  57.9 us (90%)
  local copies, waits for them, and re-layouts  4.72 us (7%)
  between operations  0.65 us (1%)
    pallas_call x1, Pallas kernels, chain(): pl.pallas_call(functools.partial(chain_kernel, n), out_shape=[jax.ShapeDt...  57.9 us
    unnamed x7, local copies, waits for them, and re-layouts  4.72 us

profile of v5, /device:TPU:31, one launch (start us, length us, event | category | flops | bytes accessed | tf_op | source)
XLA Modules:
  0.0 63.3 jit_solution(18389632352920952923)
XLA Ops:
  0.6 0.0 copy-start
  0.6 0.7 %copy-done = s32[1,8,1024]{2,1,0:T(8,128)S(1)} copy-done((s32[1,8,1024]{2,1,0:T(8,128)S(1)}, s32[1,8,1024]{2,1,0:T(8,128)}, u32[]{:S(2)}) %copy-start) | copy-done | bytes 32792
  1.4 0.0 copy-start.1
  1.4 0.7 %copy-done.1 = s32[1,8]{1,0:T(1,128)S(1)} copy-done((s32[1,8]{1,0:T(1,128)S(1)}, s32[1,8]{1,0:T(1,128)}, u32[]{:S(2)}) %copy-start.1) | copy-done | bytes 56
  2.0 57.9 %shard_map.58 = (f32[1024,1024]{1,0:T(8,128)S(1)}, f32[128,1024]{1,0:T(8,128)S(1)}, f32[1,128]{1,0:T(1,128)S(1)}) custom-call(bf16[2,1024,2048]{2,1,0:T(8,128)(2,1)} %bitcast.7, s32[8,1024]{1,0:T(8,128)S(1)} %bitcast.6, s32[1,8]{1,0:T(1,128)S(1)} %copy-done.1), custom_call_target="tpu_custom_call" | custom-call | tf_op jit(solution)/shard_map/pallas_call | solution.py:318
  59.9 2.0 %copy.9 = f32[1,1,1024,1024]{3,2,1,0:T(8,128)} copy(f32[1,1,1024,1024]{3,2,1,0:T(8,128)S(1)} %bitcast.4) | data formatting | bytes 8388608
  62.0 0.8 %copy.10 = f32[1,128,1024]{2,1,0:T(8,128)} copy(f32[1,128,1024]{2,1,0:T(8,128)S(1)} %bitcast.5) | data formatting | bytes 1048576
  62.7 0.5 copy.11
Async XLA Ops:
  0.6 0.8 %copy-start = (s32[1,8,1024]{2,1,0:T(8,128)S(1)}, s32[1,8,1024]{2,1,0:T(8,128)}, u32[]{:S(2)}) copy-start(s32[1,8,1024]{2,1,0:T(8,128)} %param.4) | copy-start | bytes 98308
  1.4 0.7 %copy-start.1 = (s32[1,8]{1,0:T(1,128)S(1)}, s32[1,8]{1,0:T(1,128)}, u32[]{:S(2)}) copy-start(s32[1,8]{1,0:T(1,128)} %channel.1) | copy-start | bytes 100
